TPU v7x, 128 devices: a whole 4x4x4 slice. The times are simulated.
128 devices in a mesh: section: 4 (over y_hi, core), frame: 32 (over y_lo, x, z).
Axes of the slice: x: 4, y: 4 (y_hi: 2, y_lo: 2; y = y_hi * 2 + y_lo), z: 4, core: 2. Of those that a mesh axis runs over, the one named last changes fastest.
Arguments:
- newcomer_groups: bfloat16 [1, 8192, 1536], P(None, 'frame'), may hold values from -6 to 6
- pending_inputs: bfloat16 [4, 8192, 1536], P('section', 'frame'), may hold values from -6 to 6
- speaker_clip_ids: int32 [5, 8192], P(None, 'frame'), may hold values from 0 to 63, never falling along the last dimension, each value on 1 to 256 neighbouring positions
- selfattend_scaling: float32 [4, 1536], P('section'), may hold values from 0.1 to 1.9
- triple_projection_matrix: bfloat16 [4, 1536, 4608], P('section', 'frame'), may hold values from -1 to 1
- selfattend_final_matrix: bfloat16 [4, 1536, 1536], P('section', 'frame'), may hold values from -0.15625 to 0.15625
- depthwise_scaling: float32 [4, 1536], P('section'), may hold values from 0.1 to 1.9
- sigmoid_expand_matrix: bfloat16 [4, 1536, 3072], P('section', 'frame'), may hold values from -0.15625 to 0.15625
- filter_taps: float32 [4, 31, 1536], P('section'), may hold values from -1 to 1
- combine_channel_matrix: bfloat16 [4, 1536, 1536], P('section', 'frame'), may hold values from -0.15625 to 0.15625
Outputs:
- section_out: bfloat16 [2, 4, 8192, 1536], P(None, 'section', 'frame')
Inputs may be any that keep to these rules, and one draw needn't show every extreme that they name: `speaker_clip_ids`: in every row the ids never fall along frames; every utterance has 1 to 256 frames, and one utterance of each row has exactly 256.
All inputs are finite; a program needn't handle non-finite values.
Results may differ from a plain program's by a relative error of at most 0.008.
Values may be sent and summed in bfloat16 or wider, within the bound.
A program may use at most 192 MiB of HBM per device.

v0:
```python
import jax
import jax.numpy as jnp
from jax import lax
from jax.sharding import PartitionSpec as P

HEADS = 24
KERNEL = 31
EPS = 1e-05


def extended(block, sides, width):
    for axis, dim in sides:
        count = lax.axis_size(axis)
        forward = [(i, i + 1) for i in range(count - 1)]
        backward = [(target, source) for source, target in forward]
        low = lax.ppermute(
            lax.slice_in_dim(block, block.shape[dim] - width, None, axis=dim), axis, forward
        )
        high = lax.ppermute(lax.slice_in_dim(block, 0, width, axis=dim), axis, backward)
        block = jnp.concatenate([low, block, high], axis=dim)
    return block


def shifted(value, axis, steps):
    count = lax.axis_size(axis)
    leading, last = (max(0, -steps), min(count, count - steps))
    return lax.ppermute(value, axis, [(source, source + steps) for source in range(leading, last)])


def layer_norm(sample_lines, gain):
    mean = jnp.mean(sample_lines, axis=-1, keepdims=True)
    centred = sample_lines - mean
    spread = jnp.mean(centred * centred, axis=-1, keepdims=True)
    return centred * lax.rsqrt(spread + EPS) * gain


def attend(query, wide_keys, wide_values, seg_wide, seg_own):
    sample_lines, feature_count = query.shape
    head_dim = feature_count // HEADS
    shaped_q = query.reshape(sample_lines, HEADS, head_dim)
    shaped_k = wide_keys.reshape(wide_keys.shape[0], HEADS, head_dim)
    shaped_v = wide_values.reshape(wide_values.shape[0], HEADS, head_dim)
    scores = jnp.einsum("qhd,khd->hqk", shaped_q, shaped_k, preferred_element_type=jnp.float32)
    allowed = (seg_own[:, None] == seg_wide[None, :])[None]
    scores = jnp.where(allowed, scores, -1e30)
    top = jnp.max(scores, axis=-1, keepdims=True)
    expd = jnp.exp(scores - top)
    probs = (expd / jnp.sum(expd, axis=-1, keepdims=True)).astype(jnp.bfloat16)
    context = jnp.einsum("hqk,khd->qhd", probs, shaped_v, preferred_element_type=jnp.float32)
    return context.astype(jnp.bfloat16).reshape(sample_lines, feature_count)


def depthwise(wide_glu, seg_conv, seg_own, taps):
    sample_lines = seg_own.shape[0]
    total = jnp.zeros((sample_lines, wide_glu.shape[1]), jnp.float32)
    for tap in range(taps.shape[0]):
        same = (seg_conv[tap : tap + sample_lines] == seg_own)[:, None]
        total = total + jnp.where(
            same, wide_glu[tap : tap + sample_lines].astype(jnp.float32) * taps[tap], 0.0
        )
    return total


def on_device(
    newcomer_groups,
    pending_inputs,
    speaker_clip_ids,
    selfattend_scaling,
    triple_projection_matrix,
    selfattend_final_matrix,
    depthwise_scaling,
    sigmoid_expand_matrix,
    filter_taps,
    combine_channel_matrix,
):
    sample_lines = pending_inputs.shape[1]
    feature_count = pending_inputs.shape[2]
    half = KERNEL // 2
    sections = lax.axis_size("section")
    section = lax.axis_index("section")
    ticks = newcomer_groups.shape[0] + 1
    seg_all = extended(speaker_clip_ids + 1, (("frame", 1),), sample_lines)
    full_qkv, full_out, full_glu, full_mix = (
        lax.all_gather(triple_projection_matrix[0], "frame", axis=0, tiled=True),
        lax.all_gather(selfattend_final_matrix[0], "frame", axis=0, tiled=True),
        lax.all_gather(sigmoid_expand_matrix[0], "frame", axis=0, tiled=True),
        lax.all_gather(combine_channel_matrix[0], "frame", axis=0, tiled=True),
    )
    present_activity = pending_inputs[0]
    made_all = []
    for tick in range(ticks):
        batch_index = sections - 1 - section + tick
        seg_wide = lax.dynamic_index_in_dim(seg_all, batch_index, 0, keepdims=False)
        seg_own = seg_wide[sample_lines : 2 * sample_lines]
        resid = present_activity.astype(jnp.float32)
        normed = layer_norm(resid, selfattend_scaling[0]).astype(jnp.bfloat16)
        projected = jnp.dot(normed, full_qkv, preferred_element_type=jnp.float32)
        query = (projected[:, :feature_count] * (feature_count // HEADS) ** (-0.5)).astype(
            jnp.bfloat16
        )
        keys = projected[:, feature_count : 2 * feature_count].astype(jnp.bfloat16)
        values = projected[:, 2 * feature_count :].astype(jnp.bfloat16)
        wide_keys, wide_values = (
            extended(keys, (("frame", 0),), sample_lines),
            extended(values, (("frame", 0),), sample_lines),
        )
        context = attend(query, wide_keys, wide_values, seg_wide, seg_own)
        resid = resid + jnp.dot(context, full_out, preferred_element_type=jnp.float32)
        conv_in = layer_norm(resid, depthwise_scaling[0]).astype(jnp.bfloat16)
        doubled = jnp.dot(conv_in, full_glu, preferred_element_type=jnp.float32)
        glu = (doubled[:, :feature_count] * jax.nn.sigmoid(doubled[:, feature_count:])).astype(
            jnp.bfloat16
        )
        wide_glu = extended(glu, (("frame", 0),), half)
        depth = depthwise(
            wide_glu,
            seg_wide[sample_lines - half : 2 * sample_lines + half],
            seg_own,
            filter_taps[0],
        )
        act = (depth * jax.nn.sigmoid(depth)).astype(jnp.bfloat16)
        resid = resid + jnp.dot(act, full_mix, preferred_element_type=jnp.float32)
        made = resid.astype(jnp.bfloat16)
        made_all.append(made)
        if tick + 1 < ticks:
            arrived = shifted(made, "section", 1)
            present_activity = jnp.where(section == 0, newcomer_groups[tick], arrived)
    return jnp.stack(made_all)[:, None]


def solution(mesh):
    in_specs = (
        P(None, "frame", None),
        P("section", "frame", None),
        P(None, "frame"),
        P("section", None),
        P("section", "frame", None),
        P("section", "frame", None),
        P("section", None),
        P("section", "frame", None),
        P("section", None, None),
        P("section", "frame", None),
    )
    out_specs = P(None, "section", "frame", None)
    return jax.shard_map(
        on_device, mesh=mesh, in_specs=in_specs, out_specs=out_specs, check_vma=False
    )
```

profile of v0, /device:TPU:118, one launch (start us, length us, event | category | flops | bytes accessed | tf_op | source)
XLA Modules:
  0.0 833.5 jit_solution(4557215190937780094)
XLA Ops:
  7.3 0.7 all-gather.11.cloned.1.call-update
  8.8 0.7 broadcast_add_fusion
  9.5 1.9 collective-permute-start.2
  11.4 3.9 collective-permute-start.3
  16.3 0.8 slice_reduce_fusion.29
  17.1 4.1 collective-permute-done.3
  21.3 0.9 fusion.163
  22.3 167.3 %all-gather.9.cloned.1.call-done = bf16[1,1536,4608]{2,1,0:T(8,128)(2,1)} async-done(((bf16[1,48,4608]{2,1,0:T(8,128)(2,1)}), bf16[1,1536,4608]{2,1,0:T(8,128)(2,1)}) %all-gather.9.cloned.1.call-update) | async-done | bytes 14155792 | tf_op jit(solution)/shard_map/all_gather | solution.py:84
  189.6 7.3 fusion.169
  196.9 1.0 fusion.159
  197.9 4.6 collective-permute-start.4
  202.5 1.9 collective-permute-start.5
  204.4 0.7 fusion.167
  205.2 0.9 broadcast_compare_fusion
  206.1 8.1 collective-permute-start
  214.2 2.2 collective-permute-start.1
  216.6 1.2 copy.19
  217.8 5.7 collective-permute-done.4
  223.5 0.9 copy-done.4
  224.4 7.2 collective-permute-done.5
  231.6 1.8 pad_maximum_fusion.1
  233.3 2.5 copy.20
  235.8 1.0 collective-permute-done
  236.8 7.7 collective-permute-done.1
  244.5 1.8 pad_maximum_fusion
  246.3 2.4 copy.18
  248.7 11.6 %fusion.170 = (f32[24,256]{1,0:T(8,128)S(1)}, f32[24,256,768]{2,1,0:T(8,128)}) fusion(pred[256,768]{1,0:T(8,128)(4,1)} %get-tuple-element.183, bf16[256,24,64]{0,2,1:T(8,128)(2,1)} %bitcast.166, bf16[768,24,64]{0,2,1:T(8,128)(2,1)} %bitcast.162), kind=kOutput, calls=%fused_computation.313 | convolution fusion | flops 618136320 | bytes 22241280 | tf_op jit(solution)/shard_map/sub | solution.py:47
  260.4 9.0 %fusion.79 = bf16[24,64,256]{2,1,0:T(8,128)(2,1)S(1)} fusion(bf16[768,24,64]{0,2,1:T(8,128)(2,1)} %bitcast.164, f32[24,256,768]{2,1,0:T(8,128)} %get-tuple-element.173, f32[24,256]{1,0:T(8,128)S(1)} %get-tuple-element.172), kind=kOutput, calls=%fused_computation.140 | convolution fusion | flops 613810176 | bytes 22044672 | tf_op jit(solution)/shard_map/hqk,khd->qhd/dot_general | solution.py:49
  269.4 83.4 %all-gather.11.cloned.1.call-done = bf16[1,1536,1536]{2,1,0:T(8,128)(2,1)} async-done(((bf16[1,48,1536]{2,1,0:T(8,128)(2,1)}), bf16[1,1536,1536]{2,1,0:T(8,128)(2,1)}) %all-gather.11.cloned.1.call-update) | async-done | bytes 4718608 | tf_op jit(solution)/shard_map/all_gather | solution.py:85
  352.7 3.8 fusion.171
  356.9 166.5 %all-gather.13.cloned.1.call-done = bf16[1,1536,3072]{2,1,0:T(8,128)(2,1)} async-done(((bf16[1,48,3072]{2,1,0:T(8,128)(2,1)}), bf16[1,1536,3072]{2,1,0:T(8,128)(2,1)}) %all-gather.13.cloned.1.call-update) | async-done | bytes 9437200 | tf_op jit(solution)/shard_map/all_gather | solution.py:86
  523.4 5.2 fusion.14
  529.2 3.6 collective-permute-start.6
  532.8 2.8 collective-permute-start.7
  536.3 148.1 %all-gather.15.cloned.1.call-done = bf16[1,1536,1536]{2,1,0:T(8,128)(2,1)} async-done(((bf16[1,48,1536]{2,1,0:T(8,128)(2,1)}), bf16[1,1536,1536]{2,1,0:T(8,128)(2,1)}) %all-gather.15.cloned.1.call-update) | async-done | bytes 4718608 | tf_op jit(solution)/shard_map/all_gather | solution.py:87
  685.1 21.7 %fusion.45 = bf16[256,1536]{1,0:T(8,128)(2,1)S(1)} fusion(f32[256,1536]{1,0:T(8,128)S(1)} %get-tuple-element.175, bf16[1,1536,1536]{2,1,0:T(8,128)(2,1)} %all-gather.15.cloned.1.call-done, bf16[256,1536]{1,0:T(8,128)(2,1)S(1)} %fusion.76, bf16[15,1536]{1,0:T(8,128)(2,1)} %copy-done.59, bf16[15,1536]{1,0:T(8,128)(2,1)} %copy-done.58, ...), kind=kOutput, calls=%fused_computation.93 | convolution fusion | flops 1294073856 | bytes 8154624 | tf_op jit(solution)/shard_map/dot_general | solution.py:122
  706.8 2.1 collective-permute-start.8
  708.9 12.7 %collective-permute-done.8 = bf16[256,1536]{1,0:T(8,128)(2,1)S(1)} collective-permute-done((bf16[256,1536]{1,0:T(8,128)(2,1)S(1)}, bf16[256,1536]{1,0:T(8,128)(2,1)S(1)}, u32[]{:S(2)}, u32[]{:S(2)}) %collective-permute-start.8) | collective-permute-done | bytes 786464 | tf_op jit(solution)/shard_map/ppermute | solution.py:27
  721.6 1.4 convert_reduce_fusion
  723.5 7.3 fusion.172
  730.8 1.0 fusion.158
  731.8 2.7 collective-permute-start.11
  734.4 3.2 collective-permute-start.12
  737.8 0.7 fusion.165
  738.5 1.9 collective-permute-start.10
  740.4 8.1 collective-permute-start.9
  748.7 1.2 copy.22
  749.9 1.0 collective-permute-done.11
  750.9 0.9 copy-done.3
  751.8 5.8 collective-permute-done.12
  757.6 1.8 pad_maximum_fusion.3
  759.4 2.5 copy.23
  761.9 4.2 collective-permute-done.10
  766.1 1.8 pad_maximum_fusion.2
  767.8 2.5 copy.21
  770.3 11.7 %fusion.173 = (f32[24,256]{1,0:T(8,128)S(1)}, f32[24,256,768]{2,1,0:T(8,128)}) fusion(pred[256,768]{1,0:T(8,128)(4,1)S(1)} %get-tuple-element.182, bf16[256,24,64]{0,2,1:T(8,128)(2,1)} %bitcast.165, bf16[768,24,64]{0,2,1:T(8,128)(2,1)} %bitcast.161), kind=kOutput, calls=%fused_computation.316 | convolution fusion | flops 618136320 | bytes 22241280 | tf_op jit(solution)/shard_map/sub | solution.py:47
  782.0 9.1 %fusion.78 = bf16[24,64,256]{2,1,0:T(8,128)(2,1)S(1)} fusion(bf16[768,24,64]{0,2,1:T(8,128)(2,1)} %bitcast.163, f32[24,256,768]{2,1,0:T(8,128)} %get-tuple-element.179, f32[24,256]{1,0:T(8,128)S(1)} %get-tuple-element.178), kind=kOutput, calls=%fused_computation.139 | convolution fusion | flops 613810176 | bytes 22044672 | tf_op jit(solution)/shard_map/hqk,khd->qhd/dot_general | solution.py:49
  791.1 1.5 fusion.174
  793.0 5.4 fusion.12
  799.2 3.4 collective-permute-start.13
  802.6 2.6 collective-permute-start.14
  805.4 7.4 collective-permute-done.14
  813.1 12.4 %fusion.48 = bf16[1,256,1536]{2,1,0:T(8,128)(2,1)S(1)} fusion(f32[256,1536]{1,0:T(8,128)S(1)} %get-tuple-element.181, bf16[1,1536,1536]{2,1,0:T(8,128)(2,1)S(1)} %bitcast.235, bf16[256,1536]{1,0:T(8,128)(2,1)S(1)} %fusion.77, bf16[15,1536]{1,0:T(8,128)(2,1)S(1)} %collective-permute-done.14, bf16[15,1536]{1,0:T(8,128)(2,1)S(1)} %collective-permute-done.13, ...), kind=kOutput, calls=%fused_computation.94 | convolution fusion | flops 1294073856 | bytes 8154624 | tf_op jit(solution)/shard_map/dot_general | solution.py:122
  825.5 1.3 maximum_bitcast_fusion
  (168 shorter events, 6.4 us)
Async XLA Ops:
  6.5 8.8 %copy-start = (bf16[1,256,1536]{2,1,0:T(8,128)(2,1)S(1)}, bf16[1,256,1536]{2,1,0:T(8,128)(2,1)}, u32[]{:S(2)}) copy-start(bf16[1,256,1536]{2,1,0:T(8,128)(2,1)} %param.11) | copy-start | bytes 2359300
  6.5 9.4 %copy-start.7 = (f32[1,31,1536]{2,0,1:T(1,128)S(1)}, f32[1,31,1536]{2,0,1:T(1,128)}, u32[]{:S(2)}) copy-start(f32[1,31,1536]{2,0,1:T(1,128)} %param.18) | copy-start | bytes 571396
  6.5 10.5 %copy-start.19 = (f32[1,1536]{1,0:T(1,128)S(1)}, f32[1,1536]{1,0:T(1,128)}, u32[]{:S(2)}) copy-start(f32[1,1536]{1,0:T(1,128)} %param.13) | copy-start | bytes 18436
  6.5 10.5 %copy-start.20 = (f32[1,1536]{1,0:T(1,128)S(1)}, f32[1,1536]{1,0:T(1,128)}, u32[]{:S(2)}) copy-start(f32[1,1536]{1,0:T(1,128)} %param.16) | copy-start | bytes 18436
  6.5 183.1 %all-gather.9.cloned.1.call-start = ((), (), s32[]{:S(2)}) async-start(), calls=%async_computation | async-start | bytes 14598144 | tf_op jit(solution)/shard_map/all_gather | solution.py:84
  7.3 345.5 %all-gather.11.cloned.1.call-start = ((), (), s32[]{:S(2)}) async-start(), calls=%async_computation.1 | async-start | bytes 4866048 | tf_op jit(solution)/shard_map/all_gather | solution.py:85
  8.0 515.3 %all-gather.13.cloned.1.call-start = ((), (), s32[]{:S(2)}) async-start(), calls=%async_computation.2 | async-start | bytes 9732096 | tf_op jit(solution)/shard_map/all_gather | solution.py:86
  8.8 675.7 %all-gather.15.cloned.1.call-start = ((), (), s32[]{:S(2)}) async-start(), calls=%async_computation.3 | async-start | bytes 4866048 | tf_op jit(solution)/shard_map/all_gather | solution.py:87
  9.5 7.6 collective-permute-start.2
  11.4 9.8 %collective-permute-start.3 = (s32[5,256]{1,0:T(8,128)S(1)}, s32[5,256]{1,0:T(8,128)S(1)}, u32[]{:S(2)}, u32[]{:S(2)}) collective-permute-start(s32[5,256]{1,0:T(8,128)S(1)} %broadcast_add_fusion), channel_id=1, source_target_pairs={{1,0},{2,1},{3,2},{4,3},{5,4},{6,5},{7,6},{8,7},{9,8},{10,9},{11,1... | collective-permute-start | bytes 15368 | tf_op jit(solution)/shard_map/ppermute | solution.py:19
  197.9 25.6 %copy-start.2 = (bf16[256,1536]{1,0:T(8,128)(2,1)}, bf16[256,1536]{1,0:T(8,128)(2,1)S(1)}, u32[]{:S(2)}) copy-start(bf16[256,1536]{1,0:T(8,128)(2,1)S(1)} %get-tuple-element.42) | copy-start | bytes 2359300
  197.9 25.6 %collective-permute-start.4 = (bf16[256,1536]{1,0:T(8,128)(2,1)S(1)}, bf16[256,1536]{1,0:T(8,128)(2,1)S(1)}, u32[]{:S(2)}, u32[]{:S(2)}) collective-permute-start(bf16[256,1536]{1,0:T(8,128)(2,1)S(1)} %get-tuple-element.42), channel_id=1, source_target_pairs={{0,1},{1,2},{2,3},{3,4},{4,5},{5,6},{6,7},{7,8},{8,9},{9,10},{10,1... | collective-permute-start | bytes 2359304 | tf_op jit(solution)/shard_map/ppermute | solution.py:16
  202.5 29.1 %collective-permute-start.5 = (bf16[256,1536]{1,0:T(8,128)(2,1)S(1)}, bf16[256,1536]{1,0:T(8,128)(2,1)}, u32[]{:S(2)}, u32[]{:S(2)}) collective-permute-start(bf16[256,1536]{1,0:T(8,128)(2,1)S(1)} %get-tuple-element.42), channel_id=1, source_target_pairs={{1,0},{2,1},{3,2},{4,3},{5,4},{6,5},{7,6},{8,7},{9,8},{10,9},{11,1... | collective-permute-start | bytes 2359304 | tf_op jit(solution)/shard_map/ppermute | solution.py:19
  206.1 30.7 %collective-permute-start = (bf16[256,1536]{1,0:T(8,128)(2,1)}, bf16[256,1536]{1,0:T(8,128)(2,1)}, u32[]{:S(2)}, u32[]{:S(2)}) collective-permute-start(bf16[256,1536]{1,0:T(8,128)(2,1)} %get-tuple-element.43), channel_id=1, source_target_pairs={{0,1},{1,2},{2,3},{3,4},{4,5},{5,6},{6,7},{7,8},{8,9},{9,10},{10,1... | collective-permute-start | bytes 2359304 | tf_op jit(solution)/shard_map/ppermute | solution.py:16
  214.2 30.3 %collective-permute-start.1 = (bf16[256,1536]{1,0:T(8,128)(2,1)}, bf16[256,1536]{1,0:T(8,128)(2,1)}, u32[]{:S(2)}, u32[]{:S(2)}) collective-permute-start(bf16[256,1536]{1,0:T(8,128)(2,1)} %get-tuple-element.43), channel_id=1, source_target_pairs={{1,0},{2,1},{3,2},{4,3},{5,4},{6,5},{7,6},{8,7},{9,8},{10,9},{11,1... | collective-permute-start | bytes 2359304 | tf_op jit(solution)/shard_map/ppermute | solution.py:19
  528.6 7.0 copy-start.34
  528.6 7.0 copy-start.35
  528.6 7.0 copy-start.36
  528.7 7.0 copy-start.37
  528.7 7.0 copy-start.38
  528.7 7.0 copy-start.39
  528.7 7.0 copy-start.40
  528.7 7.0 copy-start.41
  528.7 7.0 copy-start.42
  528.7 7.0 copy-start.43
  529.2 155.3 %collective-permute-start.6 = (bf16[15,1536]{1,0:T(8,128)(2,1)S(1)}, bf16[15,1536]{1,0:T(8,128)(2,1)S(1)}, u32[]{:S(2)}, u32[]{:S(2)}) collective-permute-start(bf16[15,1536]{1,0:T(8,128)(2,1)S(1)} %get-tuple-element.46), channel_id=1, source_target_pairs={{0,1},{1,2},{2,3},{3,4},{4,5},{5,6},{6,7},{7,8},{8,9},{9,10},{10,1... | collective-permute-start | bytes 138248 | tf_op jit(solution)/shard_map/ppermute | solution.py:16
  532.8 151.7 %collective-permute-start.7 = (bf16[15,1536]{1,0:T(8,128)(2,1)S(1)}, bf16[15,1536]{1,0:T(8,128)(2,1)S(1)}, u32[]{:S(2)}, u32[]{:S(2)}) collective-permute-start(bf16[15,1536]{1,0:T(8,128)(2,1)S(1)} %get-tuple-element.47), channel_id=1, source_target_pairs={{1,0},{2,1},{3,2},{4,3},{5,4},{6,5},{7,6},{8,7},{9,8},{10,9},{11,1... | collective-permute-start | bytes 138248 | tf_op jit(solution)/shard_map/ppermute | solution.py:19
  706.8 14.8 %collective-permute-start.8 = (bf16[256,1536]{1,0:T(8,128)(2,1)S(1)}, bf16[256,1536]{1,0:T(8,128)(2,1)S(1)}, u32[]{:S(2)}, u32[]{:S(2)}) collective-permute-start(bf16[256,1536]{1,0:T(8,128)(2,1)S(1)} %fusion.45), channel_id=1, source_target_pairs={{0,32},{32,64},{64,96},{1,33},{33,65},{65,97},{2,34},{34,66},{66,9... | collective-permute-start | bytes 2359304 | tf_op jit(solution)/shard_map/ppermute | solution.py:27
  730.8 7.0 copy-start.33
  731.8 19.1 %copy-start.1 = (bf16[256,1536]{1,0:T(8,128)(2,1)}, bf16[256,1536]{1,0:T(8,128)(2,1)S(1)}, u32[]{:S(2)}) copy-start(bf16[256,1536]{1,0:T(8,128)(2,1)S(1)} %get-tuple-element.40) | copy-start | bytes 2359300
  731.8 19.1 %collective-permute-start.11 = (bf16[256,1536]{1,0:T(8,128)(2,1)S(1)}, bf16[256,1536]{1,0:T(8,128)(2,1)S(1)}, u32[]{:S(2)}, u32[]{:S(2)}) collective-permute-start(bf16[256,1536]{1,0:T(8,128)(2,1)S(1)} %get-tuple-element.40), channel_id=1, source_target_pairs={{0,1},{1,2},{2,3},{3,4},{4,5},{5,6},{6,7},{7,8},{8,9},{9,10},{10,1... | collective-permute-start | bytes 2359304 | tf_op jit(solution)/shard_map/ppermute | solution.py:16
  734.4 23.2 %collective-permute-start.12 = (bf16[256,1536]{1,0:T(8,128)(2,1)S(1)}, bf16[256,1536]{1,0:T(8,128)(2,1)}, u32[]{:S(2)}, u32[]{:S(2)}) collective-permute-start(bf16[256,1536]{1,0:T(8,128)(2,1)S(1)} %get-tuple-element.40), channel_id=1, source_target_pairs={{1,0},{2,1},{3,2},{4,3},{5,4},{6,5},{7,6},{8,7},{9,8},{10,9},{11,1... | collective-permute-start | bytes 2359304 | tf_op jit(solution)/shard_map/ppermute | solution.py:19
  738.5 27.6 %collective-permute-start.10 = (bf16[256,1536]{1,0:T(8,128)(2,1)}, bf16[256,1536]{1,0:T(8,128)(2,1)}, u32[]{:S(2)}, u32[]{:S(2)}) collective-permute-start(bf16[256,1536]{1,0:T(8,128)(2,1)} %get-tuple-element.41), channel_id=1, source_target_pairs={{1,0},{2,1},{3,2},{4,3},{5,4},{6,5},{7,6},{8,7},{9,8},{10,9},{11,1... | collective-permute-start | bytes 2359304 | tf_op jit(solution)/shard_map/ppermute | solution.py:19
  740.4 25.6 %collective-permute-start.9 = (bf16[256,1536]{1,0:T(8,128)(2,1)}, bf16[256,1536]{1,0:T(8,128)(2,1)}, u32[]{:S(2)}, u32[]{:S(2)}) collective-permute-start(bf16[256,1536]{1,0:T(8,128)(2,1)} %get-tuple-element.41), channel_id=1, source_target_pairs={{0,1},{1,2},{2,3},{3,4},{4,5},{5,6},{6,7},{7,8},{8,9},{9,10},{10,1... | collective-permute-start | bytes 2359304 | tf_op jit(solution)/shard_map/ppermute | solution.py:16
  770.3 20.8 %slice-start = ((s8[4718592]{0:T(1024)(128)(4,1)}), s8[524288]{0:T(1024)(128)(4,1)S(1)}, s32[]{:S(2)}) async-start(s8[4718592]{0:T(1024)(128)(4,1)} %bitcast.157), calls=%async_computation.4 | async-start | bytes 1048576
  782.0 9.1 %slice-start.1 = ((s8[4718592]{0:T(1024)(128)(4,1)}), s8[4194304]{0:T(1024)(128)(4,1)S(1)}, s32[]{:S(2)}) async-start(s8[4718592]{0:T(1024)(128)(4,1)} %bitcast.157), calls=%async_computation.5 | async-start | bytes 8388608
  791.1 21.7 %slice-start.2 = ((s8[4718592]{0:T(1024)(128)(4,1)}), s8[524288]{0:T(1024)(128)(4,1)S(1)}, s32[]{:S(2)}) async-start(s8[4718592]{0:T(1024)(128)(4,1)} %bitcast.234), calls=%async_computation.6 | async-start | bytes 1048576
  793.0 19.9 %slice-start.3 = ((s8[4718592]{0:T(1024)(128)(4,1)}), s8[4194304]{0:T(1024)(128)(4,1)S(1)}, s32[]{:S(2)}) async-start(s8[4718592]{0:T(1024)(128)(4,1)} %bitcast.234), calls=%async_computation.7 | async-start | bytes 8388608
  798.5 14.3 %copy-start.8 = (f32[1536]{0:T(1024)S(1)}, f32[1536]{0:T(1024)}, u32[]{:S(2)}) copy-start(f32[1536]{0:T(1024)} %get-tuple-element.25) | copy-start | bytes 18436
  798.5 14.3 %copy-start.9 = (f32[1536]{0:T(1024)S(1)}, f32[1536]{0:T(1024)}, u32[]{:S(2)}) copy-start(f32[1536]{0:T(1024)} %get-tuple-element.26) | copy-start | bytes 18436
  798.5 14.3 %copy-start.10 = (f32[1536]{0:T(1024)S(1)}, f32[1536]{0:T(1024)}, u32[]{:S(2)}) copy-start(f32[1536]{0:T(1024)} %get-tuple-element.27) | copy-start | bytes 18436
  798.5 14.3 %copy-start.11 = (f32[1536]{0:T(1024)S(1)}, f32[1536]{0:T(1024)}, u32[]{:S(2)}) copy-start(f32[1536]{0:T(1024)} %get-tuple-element.28) | copy-start | bytes 18436
  798.5 14.3 %copy-start.12 = (f32[1536]{0:T(1024)S(1)}, f32[1536]{0:T(1024)}, u32[]{:S(2)}) copy-start(f32[1536]{0:T(1024)} %get-tuple-element.29) | copy-start | bytes 18436
  798.5 14.3 %copy-start.13 = (f32[1536]{0:T(1024)S(1)}, f32[1536]{0:T(1024)}, u32[]{:S(2)}) copy-start(f32[1536]{0:T(1024)} %get-tuple-element.30) | copy-start | bytes 18436
  798.6 14.3 %copy-start.14 = (f32[1536]{0:T(1024)S(1)}, f32[1536]{0:T(1024)}, u32[]{:S(2)}) copy-start(f32[1536]{0:T(1024)} %get-tuple-element.31) | copy-start | bytes 18436
  798.6 14.3 %copy-start.15 = (f32[1536]{0:T(1024)S(1)}, f32[1536]{0:T(1024)}, u32[]{:S(2)}) copy-start(f32[1536]{0:T(1024)} %get-tuple-element.32) | copy-start | bytes 18436
  798.6 14.3 %copy-start.16 = (f32[1536]{0:T(1024)S(1)}, f32[1536]{0:T(1024)}, u32[]{:S(2)}) copy-start(f32[1536]{0:T(1024)} %get-tuple-element.33) | copy-start | bytes 18436
  798.6 14.3 %copy-start.17 = (f32[1536]{0:T(1024)S(1)}, f32[1536]{0:T(1024)}, u32[]{:S(2)}) copy-start(f32[1536]{0:T(1024)} %get-tuple-element.34) | copy-start | bytes 18436
  798.6 14.3 %copy-start.18 = (f32[1536]{0:T(1024)S(1)}, f32[1536]{0:T(1024)}, u32[]{:S(2)}) copy-start(f32[1536]{0:T(1024)} %get-tuple-element.35) | copy-start | bytes 18436
  798.6 14.3 %copy-start.46 = (pred[256]{0:T(512)(128)(4,1)S(1)}, pred[256]{0:T(512)(128)(4,1)}, u32[]{:S(2)}) copy-start(pred[256]{0:T(512)(128)(4,1)} %get-tuple-element.116) | copy-start | bytes 772
  798.6 14.3 %copy-start.47 = (pred[256]{0:T(512)(128)(4,1)S(1)}, pred[256]{0:T(512)(128)(4,1)}, u32[]{:S(2)}) copy-start(pred[256]{0:T(512)(128)(4,1)} %get-tuple-element.117) | copy-start | bytes 772
  798.6 14.3 %copy-start.48 = (pred[256]{0:T(512)(128)(4,1)S(1)}, pred[256]{0:T(512)(128)(4,1)}, u32[]{:S(2)}) copy-start(pred[256]{0:T(512)(128)(4,1)} %get-tuple-element.118) | copy-start | bytes 772
  798.6 14.3 %copy-start.49 = (pred[256]{0:T(512)(128)(4,1)S(1)}, pred[256]{0:T(512)(128)(4,1)}, u32[]{:S(2)}) copy-start(pred[256]{0:T(512)(128)(4,1)} %get-tuple-element.119) | copy-start | bytes 772
  798.6 14.3 %copy-start.50 = (pred[256]{0:T(512)(128)(4,1)S(1)}, pred[256]{0:T(512)(128)(4,1)}, u32[]{:S(2)}) copy-start(pred[256]{0:T(512)(128)(4,1)} %get-tuple-element.120) | copy-start | bytes 772
  798.7 14.3 %copy-start.51 = (pred[256]{0:T(512)(128)(4,1)S(1)}, pred[256]{0:T(512)(128)(4,1)}, u32[]{:S(2)}) copy-start(pred[256]{0:T(512)(128)(4,1)} %get-tuple-element.121) | copy-start | bytes 772
  798.7 14.3 %copy-start.52 = (pred[256]{0:T(512)(128)(4,1)S(1)}, pred[256]{0:T(512)(128)(4,1)}, u32[]{:S(2)}) copy-start(pred[256]{0:T(512)(128)(4,1)} %get-tuple-element.122) | copy-start | bytes 772
  798.7 14.3 %copy-start.53 = (pred[256]{0:T(512)(128)(4,1)S(1)}, pred[256]{0:T(512)(128)(4,1)}, u32[]{:S(2)}) copy-start(pred[256]{0:T(512)(128)(4,1)} %get-tuple-element.123) | copy-start | bytes 772
  798.7 14.3 %copy-start.54 = (pred[256]{0:T(512)(128)(4,1)S(1)}, pred[256]{0:T(512)(128)(4,1)}, u32[]{:S(2)}) copy-start(pred[256]{0:T(512)(128)(4,1)} %get-tuple-element.124) | copy-start | bytes 772
  798.7 14.3 %copy-start.55 = (pred[256]{0:T(512)(128)(4,1)S(1)}, pred[256]{0:T(512)(128)(4,1)}, u32[]{:S(2)}) copy-start(pred[256]{0:T(512)(128)(4,1)} %get-tuple-element.125) | copy-start | bytes 772
  798.7 14.3 %copy-start.56 = (pred[256]{0:T(512)(128)(4,1)S(1)}, pred[256]{0:T(512)(128)(4,1)}, u32[]{:S(2)}) copy-start(pred[256]{0:T(512)(128)(4,1)} %get-tuple-element.126) | copy-start | bytes 772
  798.7 14.3 %copy-start.57 = (pred[256]{0:T(512)(128)(4,1)S(1)}, pred[256]{0:T(512)(128)(4,1)}, u32[]{:S(2)}) copy-start(pred[256]{0:T(512)(128)(4,1)} %get-tuple-element.127) | copy-start | bytes 772
  799.2 6.2 collective-permute-start.13
  802.6 10.2 %collective-permute-start.14 = (bf16[15,1536]{1,0:T(8,128)(2,1)S(1)}, bf16[15,1536]{1,0:T(8,128)(2,1)S(1)}, u32[]{:S(2)}, u32[]{:S(2)}) collective-permute-start(bf16[15,1536]{1,0:T(8,128)(2,1)S(1)} %get-tuple-element.45), channel_id=1, source_target_pairs={{1,0},{2,1},{3,2},{4,3},{5,4},{6,5},{7,6},{8,7},{9,8},{10,9},{11,1... | collective-permute-start | bytes 138248 | tf_op jit(solution)/shard_map/ppermute | solution.py:19
  813.1 12.4 %copy-start.6 = (bf16[256,1536]{1,0:T(8,128)(2,1)S(1)}, bf16[256,1536]{1,0:T(8,128)(2,1)}, u32[]{:S(2)}) copy-start(bf16[256,1536]{1,0:T(8,128)(2,1)} %copy-done.5) | copy-start | bytes 2359300
  (19 other events, 101.5 us)
Sparse Core Ops, SparseCore 0:
  9.0 180.5 all-gather.8
  191.2 161.4 all-gather.10
  354.4 168.9 all-gather.12
  524.9 159.5 all-gather.14
where the time goes:
time: 838 us; the launch traced here: 834 us
  waiting for transfers between devices  624 us (74%)
  matrix products  106 us (13%)
  starting transfers between devices  53.3 us (6%)
  local copies, waits for them, and re-layouts  19.3 us (2%)
  other arithmetic  16.1 us (2%)
  between operations  14.6 us (2%)
    all_gather x1, waiting for transfers between devices, on_device(): lax.all_gather(triple_projection_matrix[0], 'frame', axis=0, tiled=True)  167 us
    all_gather x1, waiting for transfers between devices, on_device(): lax.all_gather(sigmoid_expand_matrix[0], 'frame', axis=0, tiled=True)  166 us
    all_gather x1, waiting for transfers between devices, on_device(): lax.all_gather(combine_channel_matrix[0], 'frame', axis=0, tiled=True)  148 us
    all_gather x1, waiting for transfers between devices, on_device(): lax.all_gather(selfattend_final_matrix[0], 'frame', axis=0, tiled=True)  83.4 us
    ppermute x7, waiting for transfers between devices, extended(): lax.ppermute(lax.slice_in_dim(block, 0, width, axis=dim), axis, backward)  36.4 us
    dot_general x2, matrix products, on_device(): resid = resid + jnp.dot(act, full_mix, preferred_element_type=jnp.float32)  34.1 us
    ppermute x7, starting transfers between devices, extended(): lax.ppermute(lax.slice_in_dim(block, block.shape[dim] - width, None, axis...  32.5 us
    sub x2, matrix products, attend(): expd = jnp.exp(scores - top)  23.3 us
  transfers between devices with their start and end apart: 19, of which 14 were waited for; matrix products, arithmetic and copies ran while one was open for 7% of the time, Pallas kernels for 0%

commit v1 on v0

--- a/solution.py
+++ b/solution.py
@@ -82,7 +82,12 @@
     seg_all = extended(speaker_clip_ids + 1, (("frame", 1),), sample_lines)
     full_qkv, full_out, full_glu, full_mix = (
         lax.all_gather(triple_projection_matrix[0], "frame", axis=0, tiled=True),
-        lax.all_gather(selfattend_final_matrix[0], "frame", axis=0, tiled=True),
+        jnp.concatenate(
+            lax.all_to_all(
+                jnp.stack([selfattend_final_matrix[0]] * lax.axis_size("frame")), "frame", 0, 0
+            ),
+            axis=0,
+        ),
         lax.all_gather(sigmoid_expand_matrix[0], "frame", axis=0, tiled=True),
         lax.all_gather(combine_channel_matrix[0], "frame", axis=0, tiled=True),
     )

time: 838 us -> 748 us (0.89)
  waiting for transfers between devices: 624 us -> 519 us
    all_gather x1, waiting for transfers between devices: 166 us -> 73.9 us  [on_device(): lax.all_gather(sigmoid_expand_matrix[0], 'frame', axis=0, tiled=True)]
    all_gather x1 -> x0, waiting for transfers between devices: 83.4 us -> none  [on_device(): lax.all_gather(selfattend_final_matrix[0], 'frame', axis=0, tiled=True)]
    all_gather x1, waiting for transfers between devices: 167 us -> 220 us  [on_device(): lax.all_gather(triple_projection_matrix[0], 'frame', axis=0, tiled=True)]
    ppermute x7, waiting for transfers between devices: 7.82 us -> 27.4 us  [extended(): lax.ppermute(lax.slice_in_dim(block, block.shape[dim] - width, None, axis...]
  transfers between devices with their start and end apart: 19 -> 19, of which waited for: 14 -> 12; matrix products, arithmetic and copies ran while one was open for 7% -> 9% of each run, Pallas kernels for 0% -> 0%
where the time goes in v1:
time: 748 us; the launch traced here: 743 us
  waiting for transfers between devices  519 us (69%)
  matrix products  109 us (15%)
  starting transfers between devices  61.4 us (8%)
  local copies, waits for them, and re-layouts  22.9 us (3%)
  other arithmetic  16.1 us (2%)
  between operations  14.7 us (2%)
    all_gather x1, waiting for transfers between devices, on_device(): lax.all_gather(triple_projection_matrix[0], 'frame', axis=0, tiled=True)  220 us
    all_gather x1, waiting for transfers between devices, on_device(): lax.all_gather(combine_channel_matrix[0], 'frame', axis=0, tiled=True)  148 us
    all_gather x1, waiting for transfers between devices, on_device(): lax.all_gather(sigmoid_expand_matrix[0], 'frame', axis=0, tiled=True)  73.9 us
    dot_general x2, matrix products, on_device(): resid = resid + jnp.dot(act, full_mix, preferred_element_type=jnp.float32)  34.9 us
    ppermute x7, waiting for transfers between devices, extended(): lax.ppermute(lax.slice_in_dim(block, 0, width, axis=dim), axis, backward)  34.6 us
    ppermute x7, starting transfers between devices, extended(): lax.ppermute(lax.slice_in_dim(block, block.shape[dim] - width, None, axis...  33.4 us
    ppermute x7, waiting for transfers between devices, extended(): lax.ppermute(lax.slice_in_dim(block, block.shape[dim] - width, None, axis...  27.4 us
    sub x2, matrix products, attend(): expd = jnp.exp(scores - top)  24 us
  transfers between devices with their start and end apart: 19, of which 12 were waited for; matrix products, arithmetic and copies ran while one was open for 9% of the time, Pallas kernels for 0%

profile of v1, /device:TPU:118, one launch (start us, length us, event | category | flops | bytes accessed | tf_op | source)
XLA Modules:
  0.0 742.8 jit_solution(9613991202187113826)
XLA Ops:
  6.5 0.7 all-gather.7.cloned.1.call-update
  7.3 0.7 all-gather.9.cloned.1.call-update
  8.0 0.7 broadcast_add_fusion
  8.7 1.9 collective-permute-start.2
  10.6 3.9 collective-permute-start.3
  14.6 3.6 stack.12
  18.1 7.9 %all-to-all-start = ((bf16[32,48,1536]{2,1,0:T(8,128)(2,1)}), bf16[32,48,1536]{2,1,0:T(8,128)(2,1)}, u32[]{:S(2)}, u32[]{:S(2)}) async-start(bf16[32,48,1536]{2,1,0:T(8,128)(2,1)} %stack.12), calls=%async_computation | async-start | bytes 9437184 | tf_op jit(solution)/shard_map/all_to_all | solution.py:86
  27.7 0.8 slice_reduce_fusion.29
  28.8 0.9 fusion.153
  29.7 220.2 %all-gather.7.cloned.1.call-done = bf16[1,1536,4608]{2,1,0:T(8,128)(2,1)} async-done(((bf16[1,48,4608]{2,1,0:T(8,128)(2,1)}), bf16[1,1536,4608]{2,1,0:T(8,128)(2,1)}) %all-gather.7.cloned.1.call-update) | async-done | bytes 14155792 | tf_op jit(solution)/shard_map/all_gather | solution.py:84
  249.9 7.3 fusion.159
  257.2 1.0 fusion.149
  258.2 4.9 collective-permute-start.4
  263.1 1.9 collective-permute-start.5
  265.0 0.7 fusion.157
  265.8 0.9 broadcast_compare_fusion
  266.7 8.1 %collective-permute-start = (bf16[256,1536]{1,0:T(8,128)(2,1)}, bf16[256,1536]{1,0:T(8,128)(2,1)}, u32[]{:S(2)}, u32[]{:S(2)}) collective-permute-start(bf16[256,1536]{1,0:T(8,128)(2,1)} %get-tuple-element.43), channel_id=1, source_target_pairs={{0,1},{1,2},{2,3},{3,4},{4,5},{5,6},{6,7},{7,8},{8,9},{9,10},{10,1... | collective-permute-start | bytes 2359304 | tf_op jit(solution)/shard_map/ppermute | solution.py:16
  274.8 2.4 collective-permute-start.1
  277.3 1.2 copy.19
  278.5 18.4 %collective-permute-done.4 = bf16[256,1536]{1,0:T(8,128)(2,1)S(1)} collective-permute-done((bf16[256,1536]{1,0:T(8,128)(2,1)S(1)}, bf16[256,1536]{1,0:T(8,128)(2,1)S(1)}, u32[]{:S(2)}, u32[]{:S(2)}) %collective-permute-start.4) | collective-permute-done | bytes 786464 | tf_op jit(solution)/shard_map/ppermute | solution.py:16
  296.9 0.9 copy-done.5
  297.7 7.8 %collective-permute-done.5 = bf16[256,1536]{1,0:T(8,128)(2,1)} collective-permute-done((bf16[256,1536]{1,0:T(8,128)(2,1)S(1)}, bf16[256,1536]{1,0:T(8,128)(2,1)}, u32[]{:S(2)}, u32[]{:S(2)}) %collective-permute-start.5) | collective-permute-done | bytes 786464 | tf_op jit(solution)/shard_map/ppermute | solution.py:19
  305.6 1.8 pad_maximum_fusion.1
  307.3 2.5 copy.20
  309.9 8.0 %collective-permute-done = bf16[256,1536]{1,0:T(8,128)(2,1)} collective-permute-done((bf16[256,1536]{1,0:T(8,128)(2,1)}, bf16[256,1536]{1,0:T(8,128)(2,1)}, u32[]{:S(2)}, u32[]{:S(2)}) %collective-permute-start) | collective-permute-done | bytes 786464 | tf_op jit(solution)/shard_map/ppermute | solution.py:16
  317.9 9.2 %collective-permute-done.1 = bf16[256,1536]{1,0:T(8,128)(2,1)} collective-permute-done((bf16[256,1536]{1,0:T(8,128)(2,1)}, bf16[256,1536]{1,0:T(8,128)(2,1)}, u32[]{:S(2)}, u32[]{:S(2)}) %collective-permute-start.1) | collective-permute-done | bytes 786464 | tf_op jit(solution)/shard_map/ppermute | solution.py:19
  327.0 1.8 pad_maximum_fusion
  328.8 2.4 copy.18
  331.3 11.6 %fusion.160 = (f32[24,256]{1,0:T(8,128)S(1)}, f32[24,256,768]{2,1,0:T(8,128)}) fusion(pred[256,768]{1,0:T(8,128)(4,1)} %get-tuple-element.183, bf16[256,24,64]{0,2,1:T(8,128)(2,1)} %bitcast.155, bf16[768,24,64]{0,2,1:T(8,128)(2,1)} %bitcast.151), kind=kOutput, calls=%fused_computation.309 | convolution fusion | flops 618136320 | bytes 22241280 | tf_op jit(solution)/shard_map/sub | solution.py:47
  342.9 9.1 %fusion.69 = bf16[24,64,256]{2,1,0:T(8,128)(2,1)S(1)} fusion(bf16[768,24,64]{0,2,1:T(8,128)(2,1)} %bitcast.153, f32[24,256,768]{2,1,0:T(8,128)} %get-tuple-element.173, f32[24,256]{1,0:T(8,128)S(1)} %get-tuple-element.172), kind=kOutput, calls=%fused_computation.136 | convolution fusion | flops 613810176 | bytes 22044672 | tf_op jit(solution)/shard_map/hqk,khd->qhd/dot_general | solution.py:49
  352.0 3.9 fusion.161
  356.2 73.9 %all-gather.9.cloned.1.call-done = bf16[1,1536,3072]{2,1,0:T(8,128)(2,1)} async-done(((bf16[1,48,3072]{2,1,0:T(8,128)(2,1)}), bf16[1,1536,3072]{2,1,0:T(8,128)(2,1)}) %all-gather.9.cloned.1.call-update) | async-done | bytes 9437200 | tf_op jit(solution)/shard_map/all_gather | solution.py:91
  430.0 5.2 fusion.14
  435.8 4.0 collective-permute-start.6
  439.8 2.1 collective-permute-start.7
  442.7 147.6 %all-gather.11.cloned.1.call-done = bf16[1,1536,1536]{2,1,0:T(8,128)(2,1)} async-done(((bf16[1,48,1536]{2,1,0:T(8,128)(2,1)}), bf16[1,1536,1536]{2,1,0:T(8,128)(2,1)}) %all-gather.11.cloned.1.call-update) | async-done | bytes 4718608 | tf_op jit(solution)/shard_map/all_gather | solution.py:92
  590.9 22.5 %fusion.35 = bf16[256,1536]{1,0:T(8,128)(2,1)} fusion(f32[256,1536]{1,0:T(8,128)S(1)} %get-tuple-element.175, bf16[1,1536,1536]{2,1,0:T(8,128)(2,1)} %all-gather.11.cloned.1.call-done, bf16[256,1536]{1,0:T(8,128)(2,1)S(1)} %fusion.66, bf16[15,1536]{1,0:T(8,128)(2,1)} %copy-done.59, bf16[15,1536]{1,0:T(8,128)(2,1)} %copy-done.58, ...), kind=kOutput, calls=%fused_computation.89 | convolution fusion | flops 1294073856 | bytes 8154624 | tf_op jit(solution)/shard_map/dot_general | solution.py:127
  613.4 2.1 collective-permute-start.8
  615.5 12.9 %collective-permute-done.8 = bf16[256,1536]{1,0:T(8,128)(2,1)S(1)} collective-permute-done((bf16[256,1536]{1,0:T(8,128)(2,1)}, bf16[256,1536]{1,0:T(8,128)(2,1)S(1)}, u32[]{:S(2)}, u32[]{:S(2)}) %collective-permute-start.8) | collective-permute-done | bytes 786464 | tf_op jit(solution)/shard_map/ppermute | solution.py:27
  629.1 7.3 fusion.162
  636.4 1.0 fusion.148
  637.4 2.9 collective-permute-start.11
  640.3 2.9 collective-permute-start.12
  643.5 0.7 fusion.155
  644.1 1.9 collective-permute-start.10
  646.1 8.1 %collective-permute-start.9 = (bf16[256,1536]{1,0:T(8,128)(2,1)}, bf16[256,1536]{1,0:T(8,128)(2,1)}, u32[]{:S(2)}, u32[]{:S(2)}) collective-permute-start(bf16[256,1536]{1,0:T(8,128)(2,1)} %get-tuple-element.41), channel_id=1, source_target_pairs={{0,1},{1,2},{2,3},{3,4},{4,5},{5,6},{6,7},{7,8},{8,9},{9,10},{10,1... | collective-permute-start | bytes 2359304 | tf_op jit(solution)/shard_map/ppermute | solution.py:16
  654.3 1.2 copy.22
  655.5 1.0 collective-permute-done.11
  656.5 0.9 copy-done.4
  657.4 6.1 collective-permute-done.12
  663.5 1.8 pad_maximum_fusion.3
  665.3 2.5 copy.23
  667.7 4.2 collective-permute-done.10
  671.9 1.8 pad_maximum_fusion.2
  673.7 2.5 copy.21
  676.2 12.3 %fusion.163 = (f32[24,256]{1,0:T(8,128)}, f32[24,256,768]{2,1,0:T(8,128)}) fusion(pred[256,768]{1,0:T(8,128)(4,1)S(1)} %get-tuple-element.182, bf16[256,24,64]{0,2,1:T(8,128)(2,1)} %bitcast.154, bf16[768,24,64]{0,2,1:T(8,128)(2,1)} %bitcast.150), kind=kOutput, calls=%fused_computation.312 | convolution fusion | flops 618136320 | bytes 22241280 | tf_op jit(solution)/shard_map/sub | solution.py:47
  688.5 8.0 %fusion.68 = bf16[24,64,256]{2,1,0:T(8,128)(2,1)S(1)} fusion(bf16[768,24,64]{0,2,1:T(8,128)(2,1)S(1)} %bitcast.152, f32[24,256,768]{2,1,0:T(8,128)} %get-tuple-element.179, f32[24,256]{1,0:T(8,128)} %get-tuple-element.178), kind=kOutput, calls=%fused_computation.135 | convolution fusion | flops 613810176 | bytes 22044672 | tf_op jit(solution)/shard_map/hqk,khd->qhd/dot_general | solution.py:49
  696.6 3.9 fusion.164
  700.8 5.5 fusion.12
  707.1 3.4 collective-permute-start.13
  710.5 2.7 collective-permute-start.14
  713.4 7.4 collective-permute-done.14
  721.0 12.4 %fusion.38 = bf16[1,256,1536]{2,1,0:T(8,128)(2,1)S(1)} fusion(f32[256,1536]{1,0:T(8,128)S(1)} %get-tuple-element.181, bf16[1,1536,1536]{2,1,0:T(8,128)(2,1)S(1)} %bitcast.224, bf16[256,1536]{1,0:T(8,128)(2,1)S(1)} %fusion.67, bf16[15,1536]{1,0:T(8,128)(2,1)S(1)} %collective-permute-done.14, bf16[15,1536]{1,0:T(8,128)(2,1)S(1)} %collective-permute-done.13, ...), kind=kOutput, calls=%fused_computation.90 | convolution fusion | flops 1294073856 | bytes 8154624 | tf_op jit(solution)/shard_map/dot_general | solution.py:127
  733.4 2.4 maximum_bitcast_fusion
  (163 shorter events, 6.0 us)
Async XLA Ops:
  6.5 243.4 %all-gather.7.cloned.1.call-start = ((), (), s32[]{:S(2)}) async-start(), calls=%async_computation.1 | async-start | bytes 14598144 | tf_op jit(solution)/shard_map/all_gather | solution.py:84
  7.3 422.8 %all-gather.9.cloned.1.call-start = ((), (), s32[]{:S(2)}) async-start(), calls=%async_computation.2 | async-start | bytes 9732096 | tf_op jit(solution)/shard_map/all_gather | solution.py:91
  8.7 19.9 %collective-permute-start.2 = (s32[5,256]{1,0:T(8,128)S(1)}, s32[5,256]{1,0:T(8,128)S(1)}, u32[]{:S(2)}, u32[]{:S(2)}) collective-permute-start(s32[5,256]{1,0:T(8,128)S(1)} %broadcast_add_fusion), channel_id=1, source_target_pairs={{0,1},{1,2},{2,3},{3,4},{4,5},{5,6},{6,7},{7,8},{8,9},{9,10},{10,1... | collective-permute-start | bytes 15368 | tf_op jit(solution)/shard_map/ppermute | solution.py:16
  10.6 18.0 %collective-permute-start.3 = (s32[5,256]{1,0:T(8,128)S(1)}, s32[5,256]{1,0:T(8,128)S(1)}, u32[]{:S(2)}, u32[]{:S(2)}) collective-permute-start(s32[5,256]{1,0:T(8,128)S(1)} %broadcast_add_fusion), channel_id=1, source_target_pairs={{1,0},{2,1},{3,2},{4,3},{5,4},{6,5},{7,6},{8,7},{9,8},{10,9},{11,1... | collective-permute-start | bytes 15368 | tf_op jit(solution)/shard_map/ppermute | solution.py:19
  18.1 8.7 %copy-start = (bf16[1,256,1536]{2,1,0:T(8,128)(2,1)S(1)}, bf16[1,256,1536]{2,1,0:T(8,128)(2,1)}, u32[]{:S(2)}) copy-start(bf16[1,256,1536]{2,1,0:T(8,128)(2,1)} %param.11) | copy-start | bytes 2359300
  18.1 333.9 %all-to-all-start = ((bf16[32,48,1536]{2,1,0:T(8,128)(2,1)}), bf16[32,48,1536]{2,1,0:T(8,128)(2,1)}, u32[]{:S(2)}, u32[]{:S(2)}) async-start(bf16[32,48,1536]{2,1,0:T(8,128)(2,1)} %stack.12), calls=%async_computation | async-start | bytes 9437184 | tf_op jit(solution)/shard_map/all_to_all | solution.py:86
  26.1 564.2 %all-gather.11.cloned.1.call-start = ((), (), s32[]{:S(2)}) async-start(), calls=%async_computation.3 | async-start | bytes 4866048 | tf_op jit(solution)/shard_map/all_gather | solution.py:92
  258.2 20.3 %copy-start.2 = (bf16[256,1536]{1,0:T(8,128)(2,1)}, bf16[256,1536]{1,0:T(8,128)(2,1)S(1)}, u32[]{:S(2)}) copy-start(bf16[256,1536]{1,0:T(8,128)(2,1)S(1)} %get-tuple-element.42) | copy-start | bytes 2359300
  258.2 38.7 %collective-permute-start.4 = (bf16[256,1536]{1,0:T(8,128)(2,1)S(1)}, bf16[256,1536]{1,0:T(8,128)(2,1)S(1)}, u32[]{:S(2)}, u32[]{:S(2)}) collective-permute-start(bf16[256,1536]{1,0:T(8,128)(2,1)S(1)} %get-tuple-element.42), channel_id=1, source_target_pairs={{0,1},{1,2},{2,3},{3,4},{4,5},{5,6},{6,7},{7,8},{8,9},{9,10},{10,1... | collective-permute-start | bytes 2359304 | tf_op jit(solution)/shard_map/ppermute | solution.py:16
  263.1 42.5 %collective-permute-start.5 = (bf16[256,1536]{1,0:T(8,128)(2,1)S(1)}, bf16[256,1536]{1,0:T(8,128)(2,1)}, u32[]{:S(2)}, u32[]{:S(2)}) collective-permute-start(bf16[256,1536]{1,0:T(8,128)(2,1)S(1)} %get-tuple-element.42), channel_id=1, source_target_pairs={{1,0},{2,1},{3,2},{4,3},{5,4},{6,5},{7,6},{8,7},{9,8},{10,9},{11,1... | collective-permute-start | bytes 2359304 | tf_op jit(solution)/shard_map/ppermute | solution.py:19
  266.7 51.2 %collective-permute-start = (bf16[256,1536]{1,0:T(8,128)(2,1)}, bf16[256,1536]{1,0:T(8,128)(2,1)}, u32[]{:S(2)}, u32[]{:S(2)}) collective-permute-start(bf16[256,1536]{1,0:T(8,128)(2,1)} %get-tuple-element.43), channel_id=1, source_target_pairs={{0,1},{1,2},{2,3},{3,4},{4,5},{5,6},{6,7},{7,8},{8,9},{9,10},{10,1... | collective-permute-start | bytes 2359304 | tf_op jit(solution)/shard_map/ppermute | solution.py:16
  274.8 52.2 %collective-permute-start.1 = (bf16[256,1536]{1,0:T(8,128)(2,1)}, bf16[256,1536]{1,0:T(8,128)(2,1)}, u32[]{:S(2)}, u32[]{:S(2)}) collective-permute-start(bf16[256,1536]{1,0:T(8,128)(2,1)} %get-tuple-element.43), channel_id=1, source_target_pairs={{1,0},{2,1},{3,2},{4,3},{5,4},{6,5},{7,6},{8,7},{9,8},{10,9},{11,1... | collective-permute-start | bytes 2359304 | tf_op jit(solution)/shard_map/ppermute | solution.py:19
  435.3 6.7 copy-start.34
  435.3 6.7 copy-start.35
  435.8 154.4 %collective-permute-start.6 = (bf16[15,1536]{1,0:T(8,128)(2,1)S(1)}, bf16[15,1536]{1,0:T(8,128)(2,1)S(1)}, u32[]{:S(2)}, u32[]{:S(2)}) collective-permute-start(bf16[15,1536]{1,0:T(8,128)(2,1)S(1)} %get-tuple-element.46), channel_id=1, source_target_pairs={{0,1},{1,2},{2,3},{3,4},{4,5},{5,6},{6,7},{7,8},{8,9},{9,10},{10,1... | collective-permute-start | bytes 138248 | tf_op jit(solution)/shard_map/ppermute | solution.py:16
  439.8 150.5 %collective-permute-start.7 = (bf16[15,1536]{1,0:T(8,128)(2,1)S(1)}, bf16[15,1536]{1,0:T(8,128)(2,1)S(1)}, u32[]{:S(2)}, u32[]{:S(2)}) collective-permute-start(bf16[15,1536]{1,0:T(8,128)(2,1)S(1)} %get-tuple-element.47), channel_id=1, source_target_pairs={{1,0},{2,1},{3,2},{4,3},{5,4},{6,5},{7,6},{8,7},{9,8},{10,9},{11,1... | collective-permute-start | bytes 138248 | tf_op jit(solution)/shard_map/ppermute | solution.py:19
  590.9 37.5 %copy-start.6 = (bf16[1,256,1536]{2,1,0:T(8,128)(2,1)S(1)}, bf16[1,256,1536]{2,1,0:T(8,128)(2,1)}, u32[]{:S(2)}) copy-start(bf16[1,256,1536]{2,1,0:T(8,128)(2,1)} %param.10) | copy-start | bytes 2359300
  613.4 15.0 %collective-permute-start.8 = (bf16[256,1536]{1,0:T(8,128)(2,1)}, bf16[256,1536]{1,0:T(8,128)(2,1)S(1)}, u32[]{:S(2)}, u32[]{:S(2)}) collective-permute-start(bf16[256,1536]{1,0:T(8,128)(2,1)} %fusion.35), channel_id=1, source_target_pairs={{0,32},{32,64},{64,96},{1,33},{33,65},{65,97},{2,34},{34,66},{66,9... | collective-permute-start | bytes 2359304 | tf_op jit(solution)/shard_map/ppermute | solution.py:27
  636.4 7.0 copy-start.33
  637.4 18.1 %copy-start.1 = (bf16[256,1536]{1,0:T(8,128)(2,1)}, bf16[256,1536]{1,0:T(8,128)(2,1)S(1)}, u32[]{:S(2)}) copy-start(bf16[256,1536]{1,0:T(8,128)(2,1)S(1)} %get-tuple-element.40) | copy-start | bytes 2359300
  637.4 19.1 %collective-permute-start.11 = (bf16[256,1536]{1,0:T(8,128)(2,1)S(1)}, bf16[256,1536]{1,0:T(8,128)(2,1)S(1)}, u32[]{:S(2)}, u32[]{:S(2)}) collective-permute-start(bf16[256,1536]{1,0:T(8,128)(2,1)S(1)} %get-tuple-element.40), channel_id=1, source_target_pairs={{0,1},{1,2},{2,3},{3,4},{4,5},{5,6},{6,7},{7,8},{8,9},{9,10},{10,1... | collective-permute-start | bytes 2359304 | tf_op jit(solution)/shard_map/ppermute | solution.py:16
  640.3 23.2 %collective-permute-start.12 = (bf16[256,1536]{1,0:T(8,128)(2,1)S(1)}, bf16[256,1536]{1,0:T(8,128)(2,1)}, u32[]{:S(2)}, u32[]{:S(2)}) collective-permute-start(bf16[256,1536]{1,0:T(8,128)(2,1)S(1)} %get-tuple-element.40), channel_id=1, source_target_pairs={{1,0},{2,1},{3,2},{4,3},{5,4},{6,5},{7,6},{8,7},{9,8},{10,9},{11,1... | collective-permute-start | bytes 2359304 | tf_op jit(solution)/shard_map/ppermute | solution.py:19
  644.1 27.8 %collective-permute-start.10 = (bf16[256,1536]{1,0:T(8,128)(2,1)}, bf16[256,1536]{1,0:T(8,128)(2,1)}, u32[]{:S(2)}, u32[]{:S(2)}) collective-permute-start(bf16[256,1536]{1,0:T(8,128)(2,1)} %get-tuple-element.41), channel_id=1, source_target_pairs={{1,0},{2,1},{3,2},{4,3},{5,4},{6,5},{7,6},{8,7},{9,8},{10,9},{11,1... | collective-permute-start | bytes 2359304 | tf_op jit(solution)/shard_map/ppermute | solution.py:19
  646.1 25.9 %collective-permute-start.9 = (bf16[256,1536]{1,0:T(8,128)(2,1)}, bf16[256,1536]{1,0:T(8,128)(2,1)}, u32[]{:S(2)}, u32[]{:S(2)}) collective-permute-start(bf16[256,1536]{1,0:T(8,128)(2,1)} %get-tuple-element.41), channel_id=1, source_target_pairs={{0,1},{1,2},{2,3},{3,4},{4,5},{5,6},{6,7},{7,8},{8,9},{9,10},{10,1... | collective-permute-start | bytes 2359304 | tf_op jit(solution)/shard_map/ppermute | solution.py:16
  676.2 12.4 %copy-start.3 = (bf16[768,1536]{0,1:T(8,128)(2,1)S(1)}, bf16[768,1536]{0,1:T(8,128)(2,1)}, u32[]{:S(2)}) copy-start(bf16[768,1536]{0,1:T(8,128)(2,1)} %copy.21) | copy-start | bytes 7077892
  696.6 24.2 %slice-start = ((s8[4718592]{0:T(1024)(128)(4,1)}), s8[524288]{0:T(1024)(128)(4,1)S(1)}, s32[]{:S(2)}) async-start(s8[4718592]{0:T(1024)(128)(4,1)} %bitcast.223), calls=%async_computation.4 | async-start | bytes 1048576
  700.8 20.0 %slice-start.1 = ((s8[4718592]{0:T(1024)(128)(4,1)}), s8[4194304]{0:T(1024)(128)(4,1)S(1)}, s32[]{:S(2)}) async-start(s8[4718592]{0:T(1024)(128)(4,1)} %bitcast.223), calls=%async_computation.5 | async-start | bytes 8388608
  706.3 6.9 copy-start.21
  706.3 6.9 copy-start.22
  706.3 6.9 copy-start.23
  706.3 6.9 copy-start.24
  706.3 6.9 copy-start.25
  706.4 6.9 copy-start.26
  706.4 6.9 copy-start.27
  706.4 6.9 copy-start.28
  706.4 6.9 copy-start.29
  706.4 6.9 copy-start.30
  706.4 6.9 copy-start.31
  706.4 6.9 copy-start.32
  706.4 14.3 %copy-start.8 = (f32[1536]{0:T(1024)S(1)}, f32[1536]{0:T(1024)}, u32[]{:S(2)}) copy-start(f32[1536]{0:T(1024)} %get-tuple-element.25) | copy-start | bytes 18436
  706.4 14.3 %copy-start.9 = (f32[1536]{0:T(1024)S(1)}, f32[1536]{0:T(1024)}, u32[]{:S(2)}) copy-start(f32[1536]{0:T(1024)} %get-tuple-element.26) | copy-start | bytes 18436
  706.4 14.3 %copy-start.10 = (f32[1536]{0:T(1024)S(1)}, f32[1536]{0:T(1024)}, u32[]{:S(2)}) copy-start(f32[1536]{0:T(1024)} %get-tuple-element.27) | copy-start | bytes 18436
  706.5 14.3 %copy-start.11 = (f32[1536]{0:T(1024)S(1)}, f32[1536]{0:T(1024)}, u32[]{:S(2)}) copy-start(f32[1536]{0:T(1024)} %get-tuple-element.28) | copy-start | bytes 18436
  706.5 14.3 %copy-start.12 = (f32[1536]{0:T(1024)S(1)}, f32[1536]{0:T(1024)}, u32[]{:S(2)}) copy-start(f32[1536]{0:T(1024)} %get-tuple-element.29) | copy-start | bytes 18436
  706.5 14.3 %copy-start.13 = (f32[1536]{0:T(1024)S(1)}, f32[1536]{0:T(1024)}, u32[]{:S(2)}) copy-start(f32[1536]{0:T(1024)} %get-tuple-element.30) | copy-start | bytes 18436
  706.5 14.3 %copy-start.14 = (f32[1536]{0:T(1024)S(1)}, f32[1536]{0:T(1024)}, u32[]{:S(2)}) copy-start(f32[1536]{0:T(1024)} %get-tuple-element.31) | copy-start | bytes 18436
  706.5 14.3 %copy-start.15 = (f32[1536]{0:T(1024)S(1)}, f32[1536]{0:T(1024)}, u32[]{:S(2)}) copy-start(f32[1536]{0:T(1024)} %get-tuple-element.32) | copy-start | bytes 18436
  706.5 14.3 %copy-start.16 = (f32[1536]{0:T(1024)S(1)}, f32[1536]{0:T(1024)}, u32[]{:S(2)}) copy-start(f32[1536]{0:T(1024)} %get-tuple-element.33) | copy-start | bytes 18436
  706.5 14.3 %copy-start.17 = (f32[1536]{0:T(1024)S(1)}, f32[1536]{0:T(1024)}, u32[]{:S(2)}) copy-start(f32[1536]{0:T(1024)} %get-tuple-element.34) | copy-start | bytes 18436
  706.5 14.3 %copy-start.18 = (f32[1536]{0:T(1024)S(1)}, f32[1536]{0:T(1024)}, u32[]{:S(2)}) copy-start(f32[1536]{0:T(1024)} %get-tuple-element.35) | copy-start | bytes 18436
  706.5 14.3 %copy-start.46 = (pred[256]{0:T(512)(128)(4,1)S(1)}, pred[256]{0:T(512)(128)(4,1)}, u32[]{:S(2)}) copy-start(pred[256]{0:T(512)(128)(4,1)} %get-tuple-element.116) | copy-start | bytes 772
  706.5 14.3 %copy-start.47 = (pred[256]{0:T(512)(128)(4,1)S(1)}, pred[256]{0:T(512)(128)(4,1)}, u32[]{:S(2)}) copy-start(pred[256]{0:T(512)(128)(4,1)} %get-tuple-element.117) | copy-start | bytes 772
  706.6 14.3 %copy-start.48 = (pred[256]{0:T(512)(128)(4,1)S(1)}, pred[256]{0:T(512)(128)(4,1)}, u32[]{:S(2)}) copy-start(pred[256]{0:T(512)(128)(4,1)} %get-tuple-element.118) | copy-start | bytes 772
  706.6 14.3 %copy-start.49 = (pred[256]{0:T(512)(128)(4,1)S(1)}, pred[256]{0:T(512)(128)(4,1)}, u32[]{:S(2)}) copy-start(pred[256]{0:T(512)(128)(4,1)} %get-tuple-element.119) | copy-start | bytes 772
  706.6 14.3 %copy-start.50 = (pred[256]{0:T(512)(128)(4,1)S(1)}, pred[256]{0:T(512)(128)(4,1)}, u32[]{:S(2)}) copy-start(pred[256]{0:T(512)(128)(4,1)} %get-tuple-element.120) | copy-start | bytes 772
  706.6 14.3 %copy-start.51 = (pred[256]{0:T(512)(128)(4,1)S(1)}, pred[256]{0:T(512)(128)(4,1)}, u32[]{:S(2)}) copy-start(pred[256]{0:T(512)(128)(4,1)} %get-tuple-element.121) | copy-start | bytes 772
  706.6 14.3 %copy-start.52 = (pred[256]{0:T(512)(128)(4,1)S(1)}, pred[256]{0:T(512)(128)(4,1)}, u32[]{:S(2)}) copy-start(pred[256]{0:T(512)(128)(4,1)} %get-tuple-element.122) | copy-start | bytes 772
  706.6 14.3 %copy-start.53 = (pred[256]{0:T(512)(128)(4,1)S(1)}, pred[256]{0:T(512)(128)(4,1)}, u32[]{:S(2)}) copy-start(pred[256]{0:T(512)(128)(4,1)} %get-tuple-element.123) | copy-start | bytes 772
  706.6 14.3 %copy-start.54 = (pred[256]{0:T(512)(128)(4,1)S(1)}, pred[256]{0:T(512)(128)(4,1)}, u32[]{:S(2)}) copy-start(pred[256]{0:T(512)(128)(4,1)} %get-tuple-element.124) | copy-start | bytes 772
  706.6 14.3 %copy-start.55 = (pred[256]{0:T(512)(128)(4,1)S(1)}, pred[256]{0:T(512)(128)(4,1)}, u32[]{:S(2)}) copy-start(pred[256]{0:T(512)(128)(4,1)} %get-tuple-element.125) | copy-start | bytes 772
  706.6 14.3 %copy-start.56 = (pred[256]{0:T(512)(128)(4,1)S(1)}, pred[256]{0:T(512)(128)(4,1)}, u32[]{:S(2)}) copy-start(pred[256]{0:T(512)(128)(4,1)} %get-tuple-element.126) | copy-start | bytes 772
  706.6 14.3 %copy-start.57 = (pred[256]{0:T(512)(128)(4,1)S(1)}, pred[256]{0:T(512)(128)(4,1)}, u32[]{:S(2)}) copy-start(pred[256]{0:T(512)(128)(4,1)} %get-tuple-element.127) | copy-start | bytes 772
  707.1 6.3 collective-permute-start.13
  710.5 10.2 %collective-permute-start.14 = (bf16[15,1536]{1,0:T(8,128)(2,1)S(1)}, bf16[15,1536]{1,0:T(8,128)(2,1)S(1)}, u32[]{:S(2)}, u32[]{:S(2)}) collective-permute-start(bf16[15,1536]{1,0:T(8,128)(2,1)S(1)} %get-tuple-element.45), channel_id=1, source_target_pairs={{1,0},{2,1},{3,2},{4,3},{5,4},{6,5},{7,6},{8,7},{9,8},{10,9},{11,1... | collective-permute-start | bytes 138248 | tf_op jit(solution)/shard_map/ppermute | solution.py:19
  (17 other events, 75.8 us)
Sparse Core Ops, SparseCore 0:
  9.0 240.8 all-gather.6
  251.6 178.4 all-gather.8
  431.7 158.5 all-gather.10
